TPU v7x, 128 devices: a whole 4x4x4 slice. The times are simulated.
128 devices in a mesh: dp: 16 (over x, y), expert: 8 (over z, core).
Axes of the slice: x: 4, y: 4, z: 4, core: 2. Of those that a mesh axis runs over, the one named last changes fastest.
Arguments:
- tokens: bfloat16 [2048, 4096], P('dp', 'expert'), may hold values from -6 to 6
- output_gradient: bfloat16 [2048, 4096], P('dp', 'expert'), may hold values from -6 to 6
- routing: int32 [2048, 2], P('dp'), may hold values from 0 to 7, all different within a row; in each aligned block of 128 rows (0 to 127, 128 to 255, ...) at most 96 rows name the same one
- router_gate_values: float32 [2048, 2], P('dp'), may hold values from 0.1 to 0.9
- gate_weight: bfloat16 [8, 7168, 4096], P('expert', 'dp'), may hold values from -0.09375 to 0.09375
- up_weight: bfloat16 [8, 7168, 4096], P('expert', 'dp'), may hold values from -0.09375 to 0.09375
- down_weight: bfloat16 [8, 7168, 4096], P('expert', 'dp'), may hold values from -0.0625 to 0.0625
- adapter_lower_gate: bfloat16 [8, 16, 4096], P('expert'), may hold values from -0.09375 to 0.09375
- adapter_upper_gate: bfloat16 [8, 7168, 16], P('expert', 'dp'), may hold values from -0.375 to 0.375
- adapter_lower_up: bfloat16 [8, 16, 4096], P('expert'), may hold values from -0.09375 to 0.09375
- adapter_upper_up: bfloat16 [8, 7168, 16], P('expert', 'dp'), may hold values from -0.375 to 0.375
- adapter_lower_down: bfloat16 [8, 16, 7168], P('expert', None, 'dp'), may hold values from -0.0625 to 0.0625
- adapter_upper_down: bfloat16 [8, 4096, 16], P('expert'), may hold values from -0.375 to 0.375
Outputs:
- grad_x: bfloat16 [2048, 4096], P('dp', 'expert')
- grad_lora_a_gate: float32 [8, 16, 4096], P('expert')
- grad_lora_b_gate: float32 [8, 7168, 16], P('expert', 'dp')
- grad_lora_a_up: float32 [8, 16, 4096], P('expert')
- grad_lora_b_up: float32 [8, 7168, 16], P('expert', 'dp')
- grad_lora_a_down: float32 [8, 16, 7168], P('expert', None, 'dp')
- grad_lora_b_down: float32 [8, 4096, 16], P('expert')
Inputs may be any that keep to these rules, and one draw needn't show every extreme that they name: `routing`: each row names two different experts. In the rows of one dp shard (aligned blocks of 128 rows) no expert is named by more than 96 rows, and in some blocks one expert is named by exactly 96 rows.
All inputs are finite; a program needn't handle non-finite values.
Results may differ from a plain program's by a relative error of at most 0.015.
Values may be sent and summed in bfloat16 or wider, within the bound.
A program may use at most 256 MiB of HBM per device.

v0:
```python
import jax
import jax.numpy as jnp
from jax import lax
from jax.sharding import PartitionSpec as P

ADAPTER_SCALE = 2.0
NUM_CHUNKS = 2


def contract_pair(left, right, left_axis, right_axis):
    return lax.dot_general(
        left, right, (((left_axis,), (right_axis,)), ((), ())), preferred_element_type=jnp.float32
    )


def slot_numbers(route_rows, experts):
    picked = (route_rows[:, :, None] == jnp.arange(experts, dtype=jnp.int32)[None, None, :]).astype(
        jnp.int32
    )
    per_token = jnp.sum(picked, axis=1)
    earlier = jnp.cumsum(per_token, axis=0) - per_token
    return jnp.sum(earlier[:, None, :] * picked, axis=2)


def slot_sources(route_rows, positions, experts, capacity):
    tokens_here, choose = route_rows.shape
    target = (route_rows * capacity + positions).reshape(-1)
    owners = jnp.repeat(jnp.arange(tokens_here, dtype=jnp.int32), choose)
    member_ids = jnp.tile(jnp.arange(choose, dtype=jnp.int32), tokens_here)
    source = jnp.full((experts * capacity,), tokens_here, jnp.int32).at[target].set(owners)
    member = jnp.zeros((experts * capacity,), jnp.int32).at[target].set(member_ids)
    return (source, member)


def rows_backward_pass(input_rows, output_gradient_rows, params):
    (
        gate_weight,
        up_weight,
        down_weight,
        a_gate,
        gate_adapter_upper,
        a_up,
        up_adapter_upper,
        down_adapter_lower,
        b_down,
    ) = params
    gate_projected_lower = contract_pair(a_gate, input_rows, 1, 1).astype(jnp.bfloat16)
    up_projected_lower = contract_pair(a_up, input_rows, 1, 1).astype(jnp.bfloat16)
    gate_preactivation = contract_pair(
        gate_weight, input_rows, 1, 1
    ) + ADAPTER_SCALE * contract_pair(gate_adapter_upper, gate_projected_lower, 1, 0)
    up_preactivation = contract_pair(up_weight, input_rows, 1, 1) + ADAPTER_SCALE * contract_pair(
        up_adapter_upper, up_projected_lower, 1, 0
    )
    sigmoid_gate = jax.nn.sigmoid(gate_preactivation)
    silu_gate = gate_preactivation * sigmoid_gate
    hidden_units = (silu_gate * up_preactivation).astype(jnp.bfloat16)
    down_projected_lower = contract_pair(b_down, output_gradient_rows, 0, 1).astype(jnp.bfloat16)
    hidden_gradient = contract_pair(
        down_weight, output_gradient_rows, 1, 1
    ) + ADAPTER_SCALE * contract_pair(down_adapter_lower, down_projected_lower, 0, 0)
    gate_gradient = (
        hidden_gradient
        * up_preactivation
        * sigmoid_gate
        * (1.0 + gate_preactivation * (1.0 - sigmoid_gate))
    ).astype(jnp.bfloat16)
    up_gradient = (hidden_gradient * silu_gate).astype(jnp.bfloat16)
    gate_partial = contract_pair(gate_adapter_upper, gate_gradient, 0, 0).astype(jnp.bfloat16)
    up_partial = contract_pair(up_adapter_upper, up_gradient, 0, 0).astype(jnp.bfloat16)
    down_partial = contract_pair(down_adapter_lower, hidden_units, 1, 0).astype(jnp.bfloat16)
    paired_partials = jnp.concatenate([gate_partial, up_partial], 0)
    paired_factors = jnp.concatenate([a_gate, a_up], 0)
    gradient_rows_out = (
        contract_pair(gate_gradient, gate_weight, 0, 0)
        + contract_pair(up_gradient, up_weight, 0, 0)
        + ADAPTER_SCALE * contract_pair(paired_partials, paired_factors, 0, 0)
    )
    shared_slice = (
        ADAPTER_SCALE * contract_pair(gate_partial, input_rows, 1, 0),
        ADAPTER_SCALE * contract_pair(up_partial, input_rows, 1, 0),
        ADAPTER_SCALE * contract_pair(output_gradient_rows, down_partial, 0, 1),
    )
    owned_slice = (
        ADAPTER_SCALE * contract_pair(gate_gradient, gate_projected_lower, 1, 1),
        ADAPTER_SCALE * contract_pair(up_gradient, up_projected_lower, 1, 1),
        ADAPTER_SCALE * contract_pair(down_projected_lower, hidden_units, 1, 1),
    )
    return (gradient_rows_out, shared_slice, owned_slice)


def local(
    tokens,
    output_gradient,
    routing,
    router_gate_values,
    gate_weight,
    up_weight,
    down_weight,
    adapter_lower_gate,
    adapter_upper_gate,
    adapter_lower_up,
    adapter_upper_up,
    adapter_lower_down,
    adapter_upper_down,
):
    experts = lax.axis_size("expert")
    shards = lax.axis_size("dp")
    tok_local, feat_local = tokens.shape
    choose = routing.shape[1]
    complete_width = feat_local * experts
    capacity = min(tok_local, 6 * tok_local // experts)
    adapter_rank = adapter_lower_gate.shape[1]
    chunks = NUM_CHUNKS
    piece = capacity // chunks
    params = (
        gate_weight[0],
        up_weight[0],
        down_weight[0],
        adapter_lower_gate[0],
        adapter_upper_gate[0],
        adapter_lower_up[0],
        adapter_upper_up[0],
        adapter_lower_down[0],
        adapter_upper_down[0],
    )
    positions = slot_numbers(routing, experts)
    zero_row = jnp.zeros((1, feat_local), jnp.bfloat16)
    source, member = slot_sources(routing, positions, experts, capacity)
    clamped = jnp.minimum(source, tok_local - 1)
    slot_gate = jnp.where(
        source < tok_local, router_gate_values.reshape(-1)[clamped * choose + member], 0.0
    )
    send_x = jnp.concatenate([tokens, zero_row], 0)[source].reshape(experts, capacity, feat_local)
    send_dy = (
        (
            slot_gate[:, None]
            * jnp.concatenate([output_gradient, zero_row], 0)[source].astype(jnp.float32)
        )
        .astype(jnp.bfloat16)
        .reshape(experts, capacity, feat_local)
    )
    send_both = jnp.concatenate([send_x, send_dy], axis=2)
    recv_both = lax.all_to_all(send_both, "expert", split_axis=0, concat_axis=2, tiled=True)[0]
    recv_both = recv_both.reshape(capacity, experts, 2, feat_local).transpose(0, 2, 1, 3)
    recv_both = recv_both.reshape(capacity, 2 * complete_width)
    rows_pieces = []
    shared_total = None
    owned_total = None
    for c in range(chunks):
        part = recv_both[c * piece : (c + 1) * piece]
        gathered = lax.all_gather(part, "dp", axis=0, tiled=True)
        x_rows = gathered[:, :complete_width]
        dy_rows = gathered[:, complete_width:]
        rows_out, shared_slice, owned_slice = rows_backward_pass(x_rows, dy_rows, params)
        if c == 0:
            shared_total, owned_total = (shared_slice, owned_slice)
        else:
            shared_total = jax.tree.map(jnp.add, shared_total, shared_slice)
            owned_total = jax.tree.map(jnp.add, owned_total, owned_slice)
        rows_bf = rows_out.astype(jnp.bfloat16).reshape(shards, piece, complete_width)
        summed = lax.psum_scatter(rows_bf, "dp", scatter_dimension=0, tiled=True)[0]
        rows_pieces.append(summed)
    lora = jnp.concatenate([shared_total[0], shared_total[1], shared_total[2].T], 0).astype(
        jnp.bfloat16
    )
    lora_shape = lora.shape
    lora_part = lax.psum_scatter(
        lora.reshape(shards * 8, -1), "dp", scatter_dimension=0, tiled=True
    )
    summed = jnp.concatenate(rows_pieces, 0)
    lora_part = lax.optimization_barrier(lora_part)
    lora_sum = lax.all_gather(lora_part, "dp", axis=0, tiled=True).astype(jnp.float32)
    lora_sum = lora_sum.reshape(lora_shape)
    grad_a_gate = lora_sum[:adapter_rank]
    grad_a_up = lora_sum[adapter_rank : 2 * adapter_rank]
    grad_b_down = lora_sum[2 * adapter_rank :].T
    returned_rows = lax.all_to_all(
        summed.reshape(capacity, experts, feat_local),
        "expert",
        split_axis=1,
        concat_axis=1,
        tiled=True,
    ).astype(jnp.float32)
    lookup = positions * experts + routing
    grad_x = jnp.sum(returned_rows.reshape(capacity * experts, feat_local)[lookup], axis=1).astype(
        jnp.bfloat16
    )
    return (
        grad_x,
        grad_a_gate[None],
        owned_total[0][None],
        grad_a_up[None],
        owned_total[1][None],
        owned_total[2][None],
        grad_b_down[None],
    )


def solution(mesh):
    return jax.shard_map(
        local,
        mesh=mesh,
        in_specs=(
            P("dp", "expert"),
            P("dp", "expert"),
            P("dp", None),
            P("dp", None),
            P("expert", "dp", None),
            P("expert", "dp", None),
            P("expert", "dp", None),
            P("expert", None, None),
            P("expert", "dp", None),
            P("expert", None, None),
            P("expert", "dp", None),
            P("expert", None, "dp"),
            P("expert", None, None),
        ),
        out_specs=(
            P("dp", "expert"),
            P("expert", None, None),
            P("expert", "dp", None),
            P("expert", None, None),
            P("expert", "dp", None),
            P("expert", None, "dp"),
            P("expert", None, None),
        ),
        check_vma=False,
    )
```

profile of v0, /device:TPU:1, one launch (start us, length us, event | category | flops | bytes accessed | tf_op | source)
XLA Modules:
  0.0 568.4 jit_solution(9020184322485059997)
XLA Ops:
  14.7 5.0 gather_fusion.1
  19.8 2.7 gather_fusion.2
  22.5 2.7 gather_fusion
  25.7 27.4 %all_to_all.20 = bf16[8,96,1024]{2,1,0:T(8,128)(2,1)S(1)} all-to-all(bf16[8,96,1024]{2,1,0:T(8,128)(2,1)S(1)} %pad_maximum_fusion), channel_id=1, replica_groups=mesh['dp'=16,'expert'=8] {'expert'}, dimensions={0} | all-to-all | bytes 3145728 | tf_op jit(solution)/shard_map/all_to_all | solution.py:144
  60.7 88.0 %all-gather.3.cloned.1.call-done = bf16[768,8192]{1,0:T(8,128)(2,1)} async-done(((bf16[48,8192]{1,0:T(8,128)(2,1)}), bf16[768,8192]{1,0:T(8,128)(2,1)}) %all-gather.3.cloned.1.call-update) | async-done | bytes 12582928 | tf_op jit(solution)/shard_map/all_gather | solution.py:152
  148.7 4.7 fusion.79
  153.4 6.0 %fusion.31 = f32[768,448]{0,1:T(8,128)S(1)} fusion(bf16[1,448,4096]{2,1,0:T(8,128)(2,1)S(1)} %copy-done.2, bf16[768,8192]{1,0:T(8,128)(2,1)} %all-gather.3.cloned.1.call-done), kind=kOutput, calls=%fused_computation.35 | convolution fusion | flops 2818572288 | bytes 11337728 | tf_op jit(solution)/shard_map/dot_general | solution.py:11
  162.3 3.1 fusion.10
  167.9 14.7 %fusion.39 = f32[768,448]{0,1:T(8,128)S(1)} fusion(bf16[1,448,4096]{2,1,0:T(8,128)(2,1)S(1)} %copy-done.4, bf16[768,8192]{1,0:T(8,128)(2,1)S(1)} %bitcast.166), kind=kOutput, calls=%fused_computation.43 | convolution fusion | flops 2818572288 | bytes 11337728 | tf_op jit(solution)/shard_map/dot_general | solution.py:11
  184.8 6.6 %fusion.29 = f32[768,4096]{1,0:T(8,128)} fusion(bf16[448,768]{1,0:T(8,128)(2,1)S(1)} %get-tuple-element.8, bf16[1,448,4096]{2,1,0:T(8,128)(2,1)S(1)} %copy-done.2), kind=kOutput, calls=%fused_computation.33 | convolution fusion | flops 2818572288 | bytes 16941056 | tf_op jit(solution)/shard_map/dot_general | solution.py:11
  191.4 6.5 %fusion.37 = f32[768,4096]{1,0:T(8,128)} fusion(bf16[448,768]{1,0:T(8,128)(2,1)S(1)} %get-tuple-element.9, bf16[1,448,4096]{2,1,0:T(8,128)(2,1)S(1)} %copy-done.4), kind=kOutput, calls=%fused_computation.41 | convolution fusion | flops 2818572288 | bytes 16941056 | tf_op jit(solution)/shard_map/dot_general | solution.py:11
  197.9 42.7 %all-gather.5.cloned.1.call-done = bf16[768,8192]{1,0:T(8,128)(2,1)} async-done(((bf16[48,8192]{1,0:T(8,128)(2,1)}), bf16[768,8192]{1,0:T(8,128)(2,1)}) %all-gather.5.cloned.1.call-update) | async-done | bytes 12582928 | tf_op jit(solution)/shard_map/all_gather | solution.py:152
  240.5 4.7 fusion.91
  245.2 6.0 %fusion.4 = f32[768,448]{0,1:T(8,128)S(1)} fusion(bf16[768,8192]{1,0:T(8,128)(2,1)} %all-gather.5.cloned.1.call-done, bf16[1,448,4096]{2,1,0:T(8,128)(2,1)S(1)} %copy-done.35), kind=kOutput, calls=%fused_computation.12 | convolution fusion | flops 2818572288 | bytes 11337728 | tf_op jit(solution)/shard_map/dot_general | solution.py:11
  253.7 3.1 fusion.27
  259.2 3.3 fusion.35
  262.5 1.8 multiply_convert_fusion
  267.6 4.1 fusion
  271.7 4.4 fusion.23
  276.0 4.4 fusion.24
  280.4 4.1 fusion.20
  286.9 12.2 %add_convert_fusion.1 = bf16[768,4096]{1,0:T(8,128)(2,1)} fusion(f32[768,4096]{1,0:T(8,128)} %fusion.29, f32[768,4096]{1,0:T(8,128)} %fusion.37, bf16[16,4096]{1,0:T(8,128)(2,1)S(1)} %bitcast.186, bf16[16,4096]{1,0:T(8,128)(2,1)S(1)} %bitcast.184, bf16[16,768]{1,0:T(8,128)(2,1)} %bitcast.191, bf16[16,768]{1,0:T(8,128)(2,1)} %bitcast.190), kind=kOutput, calls=%fused_computation.7 | convolution fusion | flops 214532096 | bytes 31768576 | tf_op jit(solution)/shard_map/dot_general | solution.py:11
  299.2 8.9 %fusion.25 = f32[768,4096]{1,0:T(8,128)} fusion(bf16[448,768]{1,0:T(8,128)(2,1)S(1)} %get-tuple-element.11, bf16[1,448,4096]{2,1,0:T(8,128)(2,1)} %param.17), kind=kOutput, calls=%fused_computation.29 | convolution fusion | flops 2818572288 | bytes 16941056 | tf_op jit(solution)/shard_map/dot_general | solution.py:11
  308.1 6.4 %fusion.33 = f32[768,4096]{1,0:T(8,128)} fusion(bf16[448,768]{1,0:T(8,128)(2,1)S(1)} %get-tuple-element.12, bf16[1,448,4096]{2,1,0:T(8,128)(2,1)S(1)} %copy-done.6), kind=kOutput, calls=%fused_computation.37 | convolution fusion | flops 2818572288 | bytes 16941056 | tf_op jit(solution)/shard_map/dot_general | solution.py:11
  314.5 12.1 %add_convert_fusion = bf16[768,4096]{1,0:T(8,128)(2,1)} fusion(f32[768,4096]{1,0:T(8,128)} %fusion.25, f32[768,4096]{1,0:T(8,128)} %fusion.33, bf16[16,4096]{1,0:T(8,128)(2,1)S(1)} %bitcast.187, bf16[16,4096]{1,0:T(8,128)(2,1)S(1)} %bitcast.185, bf16[16,768]{1,0:T(8,128)(2,1)S(1)} %bitcast.193, bf16[16,768]{1,0:T(8,128)(2,1)S(1)} %bitcast.192), kind=kOutput, calls=%fused_computation.6 | convolution fusion | flops 214532096 | bytes 31768576 | tf_op jit(solution)/shard_map/dot_general | solution.py:11
  330.2 2.1 fusion.95
  334.8 34.6 %all-reduce.7.cloned.1.call-done = bf16[128,1536]{1,0:T(8,128)(2,1)} async-done(((bf16[128,1536]{1,0:T(8,128)(2,1)}), bf16[128,1536]{1,0:T(8,128)(2,1)}) %all-reduce.7.cloned.1.call-update) | async-done | bytes 393232
  370.1 18.3 %all_gather.11 = bf16[128,1536]{1,0:T(8,128)(2,1)S(1)} all-gather(bf16[8,1536]{1,0:T(8,128)(2,1)S(1)} %constant_dynamic-slice_fusion), channel_id=1, replica_groups=mesh['dp'=16,'expert'=8] {'dp'}, dimensions={0}, use_global_device_ids=true | all-gather | bytes 417792 | tf_op jit(solution)/shard_map/all_gather | solution.py:173
  388.9 65.0 %reduce-scatter.7.cloned.1.call-done = bf16[1,48,4096]{2,1,0:T(8,128)(2,1)} async-done(((bf16[16,48,4096]{2,1,0:T(8,128)(2,1)}), bf16[1,48,4096]{2,1,0:T(8,128)(2,1)}) %reduce-scatter.7.cloned.1.call-update) | async-done | bytes 393232
  455.1 82.5 %reduce-scatter.9.cloned.1.call-done = bf16[1,48,4096]{2,1,0:T(8,128)(2,1)} async-done(((bf16[16,48,4096]{2,1,0:T(8,128)(2,1)}), bf16[1,48,4096]{2,1,0:T(8,128)(2,1)}) %reduce-scatter.9.cloned.1.call-update) | async-done | bytes 393232
  539.9 6.2 %all-to-all-start.1 = ((bf16[96,8,512]{2,0,1:T(8,128)(2,1)}), bf16[96,8,512]{2,0,1:T(8,128)(2,1)S(1)}, u32[]{:S(2)}, u32[]{:S(2)}) async-start(bf16[96,8,512]{2,0,1:T(8,128)(2,1)} %pad_maximum_fusion.1), calls=%async_computation.1 | async-start | bytes 1572864 | tf_op jit(solution)/shard_map/all_to_all | solution.py:178
  547.0 11.4 %all-to-all-done.1 = bf16[96,8,512]{2,0,1:T(8,128)(2,1)S(1)} async-done(((bf16[96,8,512]{2,0,1:T(8,128)(2,1)}), bf16[96,8,512]{2,0,1:T(8,128)(2,1)S(1)}, u32[]{:S(2)}, u32[]{:S(2)}) %all-to-all-start.1) | async-done | bytes 786464 | tf_op jit(solution)/shard_map/all_to_all | solution.py:178
  (176 shorter events, 47.4 us)
Async XLA Ops:
  7.2 152.7 %copy-start = (bf16[1,4096,16]{1,2,0:T(8,128)(2,1)S(1)}, bf16[1,4096,16]{1,2,0:T(8,128)(2,1)}, u32[]{:S(2)}) copy-start(bf16[1,4096,16]{1,2,0:T(8,128)(2,1)} %param.25) | copy-start | bytes 393220
  7.2 12.6 %copy-start.18 = (bf16[128,512]{1,0:T(8,128)(2,1)S(1)}, bf16[128,512]{1,0:T(8,128)(2,1)}, u32[]{:S(2)}) copy-start(bf16[128,512]{1,0:T(8,128)(2,1)} %param.14) | copy-start | bytes 393220
  7.2 12.6 %copy-start.19 = (bf16[128,512]{1,0:T(8,128)(2,1)S(1)}, bf16[128,512]{1,0:T(8,128)(2,1)}, u32[]{:S(2)}) copy-start(bf16[128,512]{1,0:T(8,128)(2,1)} %param.13) | copy-start | bytes 393220
  7.2 141.5 %all-gather.3.cloned.1.call-start = ((), (), s32[]{:S(2)}) async-start(), calls=%async_computation.4 | async-start | bytes 13369344 | tf_op jit(solution)/shard_map/all_gather | solution.py:152
  57.3 91.4 %copy-start.7 = (bf16[1,16,4096]{2,1,0:T(8,128)(2,1)S(1)}, bf16[1,16,4096]{2,1,0:T(8,128)(2,1)}, u32[]{:S(2)}) copy-start(bf16[1,16,4096]{2,1,0:T(8,128)(2,1)} %param.20) | copy-start | bytes 393220
  58.8 181.7 %all-gather.5.cloned.1.call-start = ((), (), s32[]{:S(2)}) async-start(), calls=%async_computation.5 | async-start | bytes 13369344 | tf_op jit(solution)/shard_map/all_gather | solution.py:152
  60.4 309.0 %all-reduce.7.cloned.1.call-start = ((), (), s32[]{:S(2)}) async-start(), calls=%async_computation.6 | async-start | bytes 786432
  148.7 11.1 %slice-start = ((s8[12582912]{0:T(1024)(128)(4,1)}), s8[4194304]{0:T(1024)(128)(4,1)S(1)}, s32[]{:S(2)}) async-start(s8[12582912]{0:T(1024)(128)(4,1)} %bitcast.165), calls=%async_computation.9 | async-start | bytes 8388608
  153.4 6.0 %copy-start.20 = (bf16[768,16]{0,1:T(8,128)(2,1)}, bf16[768,16]{0,1:T(8,128)(2,1)S(1)}, u32[]{:S(2)}) copy-start(bf16[768,16]{0,1:T(8,128)(2,1)S(1)} %fusion.79) | copy-start | bytes 73732
  153.4 6.0 %copy-start.11 = (bf16[1,448,16]{1,2,0:T(8,128)(2,1)S(1)}, bf16[1,448,16]{1,2,0:T(8,128)(2,1)}, u32[]{:S(2)}) copy-start(bf16[1,448,16]{1,2,0:T(8,128)(2,1)} %param.21) | copy-start | bytes 43012
  153.4 6.4 %slice-start.1 = ((s8[12582912]{0:T(1024)(128)(4,1)}), s8[4194304]{0:T(1024)(128)(4,1)S(1)}, s32[]{:S(2)}) async-start(s8[12582912]{0:T(1024)(128)(4,1)} %bitcast.165), calls=%async_computation.10 | async-start | bytes 8388608
  153.4 6.4 %slice-start.2 = ((s8[12582912]{0:T(1024)(128)(4,1)}), s8[4194304]{0:T(1024)(128)(4,1)S(1)}, s32[]{:S(2)}) async-start(s8[12582912]{0:T(1024)(128)(4,1)} %bitcast.165), calls=%async_computation.11 | async-start | bytes 8388608
  167.9 14.7 %copy-start.29 = (bf16[768,16]{0,1:T(8,128)(2,1)}, bf16[768,16]{0,1:T(8,128)(2,1)S(1)}, u32[]{:S(2)}) copy-start(bf16[768,16]{0,1:T(8,128)(2,1)S(1)} %fusion.76) | copy-start | bytes 73732
  167.9 14.7 %copy-start.28 = (bf16[1,448,16]{1,2,0:T(8,128)(2,1)S(1)}, bf16[1,448,16]{1,2,0:T(8,128)(2,1)}, u32[]{:S(2)}) copy-start(bf16[1,448,16]{1,2,0:T(8,128)(2,1)} %param.23) | copy-start | bytes 43012
  184.6 80.2 %copy-start.12 = (bf16[768,16]{0,1:T(8,128)(2,1)}, bf16[768,16]{0,1:T(8,128)(2,1)S(1)}, u32[]{:S(2)}) copy-start(bf16[768,16]{0,1:T(8,128)(2,1)S(1)} %convolution_convert_fusion.5) | copy-start | bytes 73732
  184.8 81.9 %copy-start.13 = (bf16[768,16]{0,1:T(8,128)(2,1)}, bf16[768,16]{0,1:T(8,128)(2,1)S(1)}, u32[]{:S(2)}) copy-start(bf16[768,16]{0,1:T(8,128)(2,1)S(1)} %convolution_convert_fusion.4) | copy-start | bytes 73732
  240.5 11.1 %slice-start.6 = ((s8[12582912]{0:T(1024)(128)(4,1)}), s8[4194304]{0:T(1024)(128)(4,1)S(1)}, s32[]{:S(2)}) async-start(s8[12582912]{0:T(1024)(128)(4,1)} %bitcast.169), calls=%async_computation.15 | async-start | bytes 8388608
  245.2 6.0 %copy-start.26 = (bf16[768,16]{0,1:T(8,128)(2,1)}, bf16[768,16]{0,1:T(8,128)(2,1)S(1)}, u32[]{:S(2)}) copy-start(bf16[768,16]{0,1:T(8,128)(2,1)S(1)} %fusion.91) | copy-start | bytes 73732
  245.2 6.4 %slice-start.7 = ((s8[12582912]{0:T(1024)(128)(4,1)}), s8[4194304]{0:T(1024)(128)(4,1)S(1)}, s32[]{:S(2)}) async-start(s8[12582912]{0:T(1024)(128)(4,1)} %bitcast.169), calls=%async_computation.16 | async-start | bytes 8388608
  245.2 6.4 %slice-start.8 = ((s8[12582912]{0:T(1024)(128)(4,1)}), s8[4194304]{0:T(1024)(128)(4,1)S(1)}, s32[]{:S(2)}) async-start(s8[12582912]{0:T(1024)(128)(4,1)} %bitcast.169), calls=%async_computation.17 | async-start | bytes 8388608
  264.5 7.1 %copy-start.14 = (bf16[768,16]{0,1:T(8,128)(2,1)}, bf16[768,16]{0,1:T(8,128)(2,1)S(1)}, u32[]{:S(2)}) copy-start(bf16[768,16]{0,1:T(8,128)(2,1)S(1)} %convolution_convert_fusion.3) | copy-start | bytes 73732
  265.0 11.1 %copy-start.16 = (bf16[768,16]{0,1:T(8,128)(2,1)}, bf16[768,16]{0,1:T(8,128)(2,1)S(1)}, u32[]{:S(2)}) copy-start(bf16[768,16]{0,1:T(8,128)(2,1)S(1)} %convolution_convert_fusion.2) | copy-start | bytes 73732
  280.4 6.4 %copy-start.9 = (bf16[1,16,4096]{2,1,0:T(8,128)(2,1)S(1)}, bf16[1,16,4096]{2,1,0:T(8,128)(2,1)}, u32[]{:S(2)}) copy-start(bf16[1,16,4096]{2,1,0:T(8,128)(2,1)} %param.22) | copy-start | bytes 393220
  286.8 167.1 %reduce-scatter.7.cloned.1.call-start = ((), (), s32[]{:S(2)}) async-start(), calls=%async_computation.7 | async-start | bytes 6684672
  299.1 238.5 %reduce-scatter.9.cloned.1.call-start = ((), (), s32[]{:S(2)}) async-start(), calls=%async_computation.8 | async-start | bytes 6684672
  299.2 8.9 %copy-start.6 = (bf16[1,448,4096]{2,1,0:T(8,128)(2,1)S(1)}, bf16[1,448,4096]{2,1,0:T(8,128)(2,1)}, u32[]{:S(2)}) copy-start(bf16[1,448,4096]{2,1,0:T(8,128)(2,1)} %param.18) | copy-start | bytes 11010052
  308.1 6.4 %copy-start.15 = (bf16[768,16]{0,1:T(8,128)(2,1)S(1)}, bf16[768,16]{0,1:T(8,128)(2,1)}, u32[]{:S(2)}) copy-start(bf16[768,16]{0,1:T(8,128)(2,1)} %copy-done.14) | copy-start | bytes 73732
  308.1 6.4 %copy-start.17 = (bf16[768,16]{0,1:T(8,128)(2,1)S(1)}, bf16[768,16]{0,1:T(8,128)(2,1)}, u32[]{:S(2)}) copy-start(bf16[768,16]{0,1:T(8,128)(2,1)} %copy-done.16) | copy-start | bytes 73732
  326.7 5.9 %copy-start.32 = (bf16[768,16]{0,1:T(8,128)(2,1)S(1)}, bf16[768,16]{0,1:T(8,128)(2,1)}, u32[]{:S(2)}) copy-start(bf16[768,16]{0,1:T(8,128)(2,1)} %copy-done.31) | copy-start | bytes 73732
  326.7 6.9 %copy-start.21 = (bf16[768,16]{0,1:T(8,128)(2,1)S(1)}, bf16[768,16]{0,1:T(8,128)(2,1)}, u32[]{:S(2)}) copy-start(bf16[768,16]{0,1:T(8,128)(2,1)} %copy-done.20) | copy-start | bytes 73732
  326.7 7.2 %copy-start.25 = (bf16[768,16]{0,1:T(8,128)(2,1)S(1)}, bf16[768,16]{0,1:T(8,128)(2,1)}, u32[]{:S(2)}) copy-start(bf16[768,16]{0,1:T(8,128)(2,1)} %copy-done.24) | copy-start | bytes 73732
  539.9 18.5 %all-to-all-start.1 = ((bf16[96,8,512]{2,0,1:T(8,128)(2,1)}), bf16[96,8,512]{2,0,1:T(8,128)(2,1)S(1)}, u32[]{:S(2)}, u32[]{:S(2)}) async-start(bf16[96,8,512]{2,0,1:T(8,128)(2,1)} %pad_maximum_fusion.1), calls=%async_computation.1 | async-start | bytes 1572864 | tf_op jit(solution)/shard_map/all_to_all | solution.py:178
  (20 other events, 63.6 us)
Sparse Core Ops, SparseCore 0:
  58.9 89.7 all-gather.2
  150.9 89.5 all-gather.4
  286.9 82.4 all-reduce.6
  372.7 81.1 reduce-scatter.6
  457.2 80.4 reduce-scatter.8
where the time goes:
time: 576 us; the launch traced here: 568 us
  waiting for transfers between devices  324 us (56%)
  matrix products  136 us (24%)
  blocking collectives  45.7 us (8%)
  local copies, waits for them, and re-layouts  33 us (6%)
  between operations  15.6 us (3%)
  other arithmetic  6.67 us (1%)
  starting transfers between devices  6.65 us (1%)
    unnamed x8, waiting for transfers between devices  182 us
    dot_general x40, matrix products, contract_pair(): lax.dot_general(left, right, (((left_axis,), (right_axis,)), ((), ())), p...  136 us
    all_gather x2, waiting for transfers between devices, local(): gathered = lax.all_gather(part, 'dp', axis=0, tiled=True)  131 us
    all_to_all x1, blocking collectives, local(): lax.all_to_all(send_both, 'expert', split_axis=0, concat_axis=2, tiled=True)  27.4 us
    all_gather x1, blocking collectives, local(): lax.all_gather(lora_part, 'dp', axis=0, tiled=True).astype(jnp.float32)  18.3 us
  transfers between devices with their start and end apart: 6, of which 6 were waited for; matrix products, arithmetic and copies ran while one was open for 17% of the time, Pallas kernels for 0%

commit v1 on v0

--- a/solution.py
+++ b/solution.py
@@ -5,6 +5,12 @@
 
 ADAPTER_SCALE = 2.0
 NUM_CHUNKS = 2
+
+
+def gather_from_all(x, axis, dim):
+    size = lax.axis_size(axis)
+    repeats = [size if d == dim else 1 for d in range(x.ndim)]
+    return lax.all_to_all(jnp.tile(x, repeats), axis, split_axis=dim, concat_axis=dim, tiled=True)
 
 
 def contract_pair(left, right, left_axis, right_axis):
@@ -149,7 +155,7 @@
     owned_total = None
     for c in range(chunks):
         part = recv_both[c * piece : (c + 1) * piece]
-        gathered = lax.all_gather(part, "dp", axis=0, tiled=True)
+        gathered = gather_from_all(part, "dp", 0)
         x_rows = gathered[:, :complete_width]
         dy_rows = gathered[:, complete_width:]
         rows_out, shared_slice, owned_slice = rows_backward_pass(x_rows, dy_rows, params)

time: 576 us -> 919 us (1.60)
  waiting for transfers between devices: 324 us -> 622 us
  starting transfers between devices: 6.65 us -> 25.7 us
  matrix products: 136 us -> 153 us
    all_to_all x0 -> x2, waiting for transfers between devices: none -> 415 us  [gather_from_all(): lax.all_to_all(jnp.tile(x, repeats), axis, split_axis=dim, concat_axis=di...]
    all_gather x2 -> x0, waiting for transfers between devices: 131 us -> none  [local(): gathered = lax.all_gather(part, 'dp', axis=0, tiled=True)]
    all_to_all x0 -> x2, starting transfers between devices: none -> 19.1 us  [gather_from_all(): lax.all_to_all(jnp.tile(x, repeats), axis, split_axis=dim, concat_axis=di...]
    dot_general x40, matrix products: 136 us -> 153 us  [contract_pair(): lax.dot_general(left, right, (((left_axis,), (right_axis,)), ((), ())), p...]
    unnamed x8 -> x6, waiting for transfers between devices: 182 us -> 195 us
    another operation x0 -> x2, local copies, waits for them, and re-layouts: none -> 12.2 us  [gather_from_all(): jnp.tile(x, repeats)]
  transfers between devices with their start and end apart: 6 -> 6, of which waited for: 6 -> 6; matrix products, arithmetic and copies ran while one was open for 17% -> 7% of each run, Pallas kernels for 0% -> 0%
where the time goes in v1:
time: 919 us; the launch traced here: 910 us
  waiting for transfers between devices  622 us (68%)
  matrix products  153 us (17%)
  blocking collectives  45.5 us (5%)
  local copies, waits for them, and re-layouts  41.5 us (5%)
  starting transfers between devices  25.7 us (3%)
  between operations  15.2 us (2%)
    all_to_all x2, waiting for transfers between devices, gather_from_all(): lax.all_to_all(jnp.tile(x, repeats), axis, split_axis=dim, concat_axis=di...  415 us
    unnamed x6, waiting for transfers between devices  195 us
    dot_general x40, matrix products, contract_pair(): lax.dot_general(left, right, (((left_axis,), (right_axis,)), ((), ())), p...  153 us
    all_to_all x1, blocking collectives, local(): lax.all_to_all(send_both, 'expert', split_axis=0, concat_axis=2, tiled=True)  27.4 us
    all_to_all x2, starting transfers between devices, gather_from_all(): lax.all_to_all(jnp.tile(x, repeats), axis, split_axis=dim, concat_axis=di...  19.1 us
  transfers between devices with their start and end apart: 6, of which 6 were waited for; matrix products, arithmetic and copies ran while one was open for 7% of the time, Pallas kernels for 0%

profile of v1, /device:TPU:1, one launch (start us, length us, event | category | flops | bytes accessed | tf_op | source)
XLA Modules:
  0.0 910.0 jit_solution(1147022618846920397)
XLA Ops:
  14.6 5.0 gather_fusion.1
  25.5 27.4 %all_to_all.38 = bf16[8,96,1024]{2,1,0:T(8,128)(2,1)S(1)} all-to-all(bf16[8,96,1024]{2,1,0:T(8,128)(2,1)S(1)} %pad_maximum_fusion), channel_id=1, replica_groups=mesh['dp'=16,'expert'=8] {'expert'}, dimensions={0} | all-to-all | bytes 3145728 | tf_op jit(solution)/shard_map/all_to_all | solution.py:150
  57.7 6.1 tile.30
  63.8 6.8 all-to-all-start.1
  71.2 218.9 %all-to-all-done.1 = bf16[16,48,8192]{2,1,0:T(8,128)(2,1)} async-done(((bf16[16,48,8192]{2,1,0:T(8,128)(2,1)}), bf16[16,48,8192]{2,1,0:T(8,128)(2,1)}, u32[]{:S(2)}, u32[]{:S(2)}) %all-to-all-start.1) | async-done | bytes 12582944 | tf_op jit(solution)/shard_map/all_to_all | solution.py:13
  290.1 6.2 tile.32
  296.3 12.3 %all-to-all-start.2 = ((bf16[16,48,8192]{2,1,0:T(8,128)(2,1)}), bf16[16,48,8192]{2,1,0:T(8,128)(2,1)}, u32[]{:S(2)}, u32[]{:S(2)}) async-start(bf16[16,48,8192]{2,1,0:T(8,128)(2,1)} %tile.32), calls=%async_computation.2 | async-start | bytes 25165824 | tf_op jit(solution)/shard_map/all_to_all | solution.py:13
  308.8 4.7 fusion.88
  313.5 5.8 fusion.10
  319.3 196.6 %all-to-all-done.2 = bf16[16,48,8192]{2,1,0:T(8,128)(2,1)} async-done(((bf16[16,48,8192]{2,1,0:T(8,128)(2,1)}), bf16[16,48,8192]{2,1,0:T(8,128)(2,1)}, u32[]{:S(2)}, u32[]{:S(2)}) %all-to-all-start.2) | async-done | bytes 12582944 | tf_op jit(solution)/shard_map/all_to_all | solution.py:13
  515.9 4.7 fusion.91
  520.6 5.9 fusion.4
  526.5 4.5 fusion.79
  531.0 4.7 fusion.85
  535.7 6.1 fusion.31
  541.8 5.9 fusion.27
  547.6 4.5 fusion.76
  552.1 4.7 fusion.82
  556.8 5.8 fusion.39
  562.7 5.8 fusion.35
  571.8 6.4 fusion.29
  578.4 6.4 fusion.37
  616.7 12.0 %add_convert_fusion.1 = bf16[768,4096]{1,0:T(8,128)(2,1)} fusion(f32[768,4096]{1,0:T(8,128)} %fusion.29, f32[768,4096]{1,0:T(8,128)} %fusion.37, bf16[16,4096]{1,0:T(8,128)(2,1)S(1)} %bitcast.182, bf16[16,4096]{1,0:T(8,128)(2,1)S(1)} %bitcast.180, bf16[16,768]{1,0:T(8,128)(2,1)} %bitcast.188, bf16[16,768]{1,0:T(8,128)(2,1)} %bitcast.187), kind=kOutput, calls=%fused_computation.7 | convolution fusion | flops 214532096 | bytes 31768576 | tf_op jit(solution)/shard_map/dot_general | solution.py:17
  628.7 8.6 fusion.25
  637.4 6.4 fusion.33
  643.8 12.0 %add_convert_fusion = bf16[768,4096]{1,0:T(8,128)(2,1)} fusion(f32[768,4096]{1,0:T(8,128)} %fusion.25, f32[768,4096]{1,0:T(8,128)} %fusion.33, bf16[16,4096]{1,0:T(8,128)(2,1)S(1)} %bitcast.183, bf16[16,4096]{1,0:T(8,128)(2,1)S(1)} %bitcast.181, bf16[16,768]{1,0:T(8,128)(2,1)S(1)} %bitcast.189, bf16[16,768]{1,0:T(8,128)(2,1)S(1)} %bitcast.186), kind=kOutput, calls=%fused_computation.6 | convolution fusion | flops 214532096 | bytes 31768576 | tf_op jit(solution)/shard_map/dot_general | solution.py:17
  663.9 46.9 %all-reduce.7.cloned.1.call-done = bf16[128,1536]{1,0:T(8,128)(2,1)} async-done(((bf16[128,1536]{1,0:T(8,128)(2,1)}), bf16[128,1536]{1,0:T(8,128)(2,1)}) %all-reduce.7.cloned.1.call-update) | async-done | bytes 393232
  711.5 18.1 %all_gather.3 = bf16[128,1536]{1,0:T(8,128)(2,1)S(1)} all-gather(bf16[8,1536]{1,0:T(8,128)(2,1)S(1)} %constant_dynamic-slice_fusion), channel_id=1, replica_groups=mesh['dp'=16,'expert'=8] {'dp'}, dimensions={0}, use_global_device_ids=true | all-gather | bytes 417792 | tf_op jit(solution)/shard_map/all_gather | solution.py:179
  730.0 65.5 %reduce-scatter.7.cloned.1.call-done = bf16[1,48,4096]{2,1,0:T(8,128)(2,1)} async-done(((bf16[16,48,4096]{2,1,0:T(8,128)(2,1)}), bf16[1,48,4096]{2,1,0:T(8,128)(2,1)}) %reduce-scatter.7.cloned.1.call-update) | async-done | bytes 393232
  796.8 82.8 %reduce-scatter.9.cloned.1.call-done = bf16[1,48,4096]{2,1,0:T(8,128)(2,1)} async-done(((bf16[16,48,4096]{2,1,0:T(8,128)(2,1)}), bf16[1,48,4096]{2,1,0:T(8,128)(2,1)}) %reduce-scatter.9.cloned.1.call-update) | async-done | bytes 393232
  881.8 6.2 all-to-all-start.3
  888.8 11.4 %all-to-all-done.3 = bf16[96,8,512]{2,0,1:T(8,128)(2,1)S(1)} async-done(((bf16[96,8,512]{2,0,1:T(8,128)(2,1)}), bf16[96,8,512]{2,0,1:T(8,128)(2,1)S(1)}, u32[]{:S(2)}, u32[]{:S(2)}) %all-to-all-start.3) | async-done | bytes 786464 | tf_op jit(solution)/shard_map/all_to_all | solution.py:184
  (149 shorter events, 70.1 us)
Async XLA Ops:
  7.2 301.6 %copy-start = (bf16[1,4096,16]{1,2,0:T(8,128)(2,1)S(1)}, bf16[1,4096,16]{1,2,0:T(8,128)(2,1)}, u32[]{:S(2)}) copy-start(bf16[1,4096,16]{1,2,0:T(8,128)(2,1)} %param.25) | copy-start | bytes 393220
  7.2 12.4 %copy-start.15 = (bf16[128,512]{1,0:T(8,128)(2,1)S(1)}, bf16[128,512]{1,0:T(8,128)(2,1)}, u32[]{:S(2)}) copy-start(bf16[128,512]{1,0:T(8,128)(2,1)} %param.14) | copy-start | bytes 393220
  7.2 12.5 %copy-start.16 = (bf16[128,512]{1,0:T(8,128)(2,1)S(1)}, bf16[128,512]{1,0:T(8,128)(2,1)}, u32[]{:S(2)}) copy-start(bf16[128,512]{1,0:T(8,128)(2,1)} %param.13) | copy-start | bytes 393220
  63.8 226.3 %all-to-all-start.1 = ((bf16[16,48,8192]{2,1,0:T(8,128)(2,1)}), bf16[16,48,8192]{2,1,0:T(8,128)(2,1)}, u32[]{:S(2)}, u32[]{:S(2)}) async-start(bf16[16,48,8192]{2,1,0:T(8,128)(2,1)} %tile.30), calls=%async_computation.1 | async-start | bytes 25165824 | tf_op jit(solution)/shard_map/all_to_all | solution.py:13
  296.3 219.6 %all-to-all-start.2 = ((bf16[16,48,8192]{2,1,0:T(8,128)(2,1)}), bf16[16,48,8192]{2,1,0:T(8,128)(2,1)}, u32[]{:S(2)}, u32[]{:S(2)}) async-start(bf16[16,48,8192]{2,1,0:T(8,128)(2,1)} %tile.32), calls=%async_computation.2 | async-start | bytes 25165824 | tf_op jit(solution)/shard_map/all_to_all | solution.py:13
  308.6 402.2 %all-reduce.7.cloned.1.call-start = ((), (), s32[]{:S(2)}) async-start(), calls=%async_computation.6 | async-start | bytes 786432
  308.8 4.7 copy-start.31
  313.5 255.5 %copy-start.21 = (bf16[768,16]{0,1:T(8,128)(2,1)}, bf16[768,16]{0,1:T(8,128)(2,1)S(1)}, u32[]{:S(2)}) copy-start(bf16[768,16]{0,1:T(8,128)(2,1)S(1)} %fusion.88) | copy-start | bytes 73732
  515.9 4.7 copy-start.32
  520.6 67.9 %copy-start.23 = (bf16[768,16]{0,1:T(8,128)(2,1)}, bf16[768,16]{0,1:T(8,128)(2,1)S(1)}, u32[]{:S(2)}) copy-start(bf16[768,16]{0,1:T(8,128)(2,1)S(1)} %fusion.91) | copy-start | bytes 73732
  520.6 5.9 copy-start.6
  531.0 37.6 %copy-start.19 = (bf16[768,16]{0,1:T(8,128)(2,1)}, bf16[768,16]{0,1:T(8,128)(2,1)S(1)}, u32[]{:S(2)}) copy-start(bf16[768,16]{0,1:T(8,128)(2,1)S(1)} %fusion.79) | copy-start | bytes 73732
  531.0 4.7 copy-start.2
  535.7 53.2 %copy-start.17 = (bf16[768,16]{0,1:T(8,128)(2,1)}, bf16[768,16]{0,1:T(8,128)(2,1)S(1)}, u32[]{:S(2)}) copy-start(bf16[768,16]{0,1:T(8,128)(2,1)S(1)} %fusion.85) | copy-start | bytes 73732
  541.7 5.9 copy-start.7
  552.1 17.7 %copy-start.28 = (bf16[768,16]{0,1:T(8,128)(2,1)}, bf16[768,16]{0,1:T(8,128)(2,1)S(1)}, u32[]{:S(2)}) copy-start(bf16[768,16]{0,1:T(8,128)(2,1)S(1)} %fusion.76) | copy-start | bytes 73732
  552.1 4.7 copy-start.3
  556.8 32.5 %copy-start.26 = (bf16[768,16]{0,1:T(8,128)(2,1)}, bf16[768,16]{0,1:T(8,128)(2,1)S(1)}, u32[]{:S(2)}) copy-start(bf16[768,16]{0,1:T(8,128)(2,1)S(1)} %fusion.82) | copy-start | bytes 73732
  562.7 5.9 copy-start.9
  562.7 6.3 copy-start.8
  571.8 13.0 %copy-start.11 = (bf16[768,16]{0,1:T(8,128)(2,1)}, bf16[768,16]{0,1:T(8,128)(2,1)S(1)}, u32[]{:S(2)}) copy-start(bf16[768,16]{0,1:T(8,128)(2,1)S(1)} %convolution_convert_fusion.5) | copy-start | bytes 73732
  578.4 13.5 %copy-start.12 = (bf16[768,16]{0,1:T(8,128)(2,1)}, bf16[768,16]{0,1:T(8,128)(2,1)S(1)}, u32[]{:S(2)}) copy-start(bf16[768,16]{0,1:T(8,128)(2,1)S(1)} %convolution_convert_fusion.4) | copy-start | bytes 73732
  616.4 179.1 %reduce-scatter.7.cloned.1.call-start = ((), (), s32[]{:S(2)}) async-start(), calls=%async_computation.7 | async-start | bytes 6684672
  628.7 250.9 %reduce-scatter.9.cloned.1.call-start = ((), (), s32[]{:S(2)}) async-start(), calls=%async_computation.8 | async-start | bytes 6684672
  628.7 8.7 copy-start.4
  637.4 6.4 copy-start.10
  637.4 6.4 copy-start.14
  655.8 5.6 copy-start.29
  655.8 5.9 copy-start.27
  655.8 6.8 copy-start.20
  655.8 7.1 copy-start.18
  881.8 18.5 %all-to-all-start.3 = ((bf16[96,8,512]{2,0,1:T(8,128)(2,1)}), bf16[96,8,512]{2,0,1:T(8,128)(2,1)S(1)}, u32[]{:S(2)}, u32[]{:S(2)}) async-start(bf16[96,8,512]{2,0,1:T(8,128)(2,1)} %pad_maximum_fusion.1), calls=%async_computation.3 | async-start | bytes 1572864 | tf_op jit(solution)/shard_map/all_to_all | solution.py:184
  (8 other events, 20.3 us)
Sparse Core Ops, SparseCore 0:
  616.5 94.1 all-reduce.6
  714.2 81.3 reduce-scatter.6
  799.0 80.5 reduce-scatter.8
